TPU v7x, 32 devices: a whole 2x2x4 slice. The times are simulated.
32 devices in a mesh: gy: 8 (over y, x, core), gz: 4 (over z).
Axes of the slice: x: 2, y: 2, z: 4, core: 2. Of those that a mesh axis runs over, the one named last changes fastest.
Arguments:
- volume: float32 [64, 128, 1024], P('gz', None, 'gy'), may hold values from -6 to 6
- contrast: float32 [128], replicated, may hold values from 0.1 to 1
Outputs:
- filtered: float32 [64, 128, 1024], P('gz', None, 'gy')
All inputs are finite; a program needn't handle non-finite values.
Results may differ from a plain program's by a relative error of at most 0.0003.
Values sent between devices are 32-bit elements; how exact they have to be, the bound alone decides.
A program may use at most 192 MiB of HBM per device.

v0:
```python
import jax
import jax.numpy as jnp
from jax import lax
from jax.sharding import PartitionSpec as P

STEPS = 2
kernel_taps = (0.05448868, 0.24420134, 0.40261995, 0.24420134, 0.05448868)
half_scale = 600.0


def extended(block, sides, width):
    for axis, dim in sides:
        count = lax.axis_size(axis)
        forward = [(i, i + 1) for i in range(count - 1)]
        backward = [(target, source) for source, target in forward]
        low = lax.ppermute(
            lax.slice_in_dim(block, block.shape[dim] - width, None, axis=dim), axis, forward
        )
        high = lax.ppermute(lax.slice_in_dim(block, 0, width, axis=dim), axis, backward)
        block = jnp.concatenate([low, block, high], axis=dim)
    return block


def slice_axis(array, start, count, axis, stride=1):
    return lax.slice_in_dim(array, start, start + stride * (count - 1) + 1, stride, axis)


def reduce_solve(lower, diagonal, upper, right, axis):
    length = right.shape[axis]
    if length == 1:
        return right / diagonal
    count_even = (length + 1) // 2
    count_odd = length // 2
    evens = [slice_axis(array, 0, count_even, axis, 2) for array in (lower, diagonal, upper, right)]
    odds = [slice_axis(array, 1, count_odd, axis, 2) for array in (lower, diagonal, upper, right)]
    before = [slice_axis(array, 0, count_odd, axis) for array in evens]
    fills = [0.0, 1.0, 0.0, 0.0]
    after = [
        slice_axis(
            jnp.concatenate([array, jnp.zeros_like(slice_axis(array, 0, 1, axis)) + extra], axis),
            1,
            count_odd,
            axis,
        )
        for array, extra in zip(evens, fills)
    ]
    factor_before = -odds[0] / before[1]
    factor_after = -odds[2] / after[1]
    new_lower = factor_before * before[0]
    new_diag = odds[1] + factor_before * before[2] + factor_after * after[0]
    new_upper = factor_after * after[2]
    new_right = odds[3] + factor_before * before[3] + factor_after * after[3]
    solved_odd = reduce_solve(new_lower, new_diag, new_upper, new_right, axis)
    zero_row = jnp.zeros_like(slice_axis(solved_odd, 0, 1, axis))
    extra_rows = [zero_row] * (count_even - count_odd)
    padded_odd = jnp.concatenate([zero_row, solved_odd] + extra_rows, axis)
    left_value = slice_axis(padded_odd, 0, count_even, axis)
    right_value = slice_axis(padded_odd, 1, count_even, axis)
    solved_even = (evens[3] - evens[0] * left_value - evens[2] * right_value) / evens[1]
    odd_full = jnp.concatenate([solved_odd] + extra_rows, axis)
    paired = jnp.stack([solved_even, odd_full], axis=axis + 1)
    shape = right.shape[:axis] + (2 * count_even,) + right.shape[axis + 1 :]
    return slice_axis(paired.reshape(shape), 0, length, axis)


def line_solve(upper, right, axis):
    length = upper.shape[axis]
    lower = jnp.concatenate(
        [jnp.zeros_like(slice_axis(upper, 0, 1, axis)), slice_axis(upper, 0, length - 1, axis)],
        axis,
    )
    diagonal = 1.0 + lower + upper
    return reduce_solve(-lower, diagonal, -upper, right, axis)


def smooth_axis(padded, axis):
    count = padded.shape[axis] - 4
    total = kernel_taps[0] * slice_axis(padded, 0, count, axis)
    for offset in range(1, 5):
        total = total + kernel_taps[offset] * slice_axis(padded, offset, count, axis)
    return total


def on_device(volume, contrast):
    depth, rows, cols = volume.shape
    count_z = lax.axis_size("gz")
    count_y = lax.axis_size("gy")
    total_z = depth * count_z
    total_y = cols * count_y
    start_z = lax.axis_index("gz") * depth
    start_y = lax.axis_index("gy") * cols
    pos_z = start_z - 2 + jnp.arange(depth + 4)
    pos_y = start_y - 2 + jnp.arange(cols + 4)
    inside = ((pos_z >= 0) & (pos_z < total_z))[:, None, None] & ((pos_y >= 0) & (pos_y < total_y))[
        None, None, :
    ]
    own_z = start_z + jnp.arange(depth) < total_z - 1
    own_y = start_y + jnp.arange(cols) < total_y - 1
    contrast_squared = (contrast * contrast)[None, :, None]
    current = volume
    for repeat in range(STEPS):
        padded = extended(current, (("gy", 2), ("gz", 0)), 4)
        blurred = smooth_axis(padded, 0)
        blurred = smooth_axis(blurred, 2)
        blurred = smooth_axis(jnp.pad(blurred, ((0, 0), (2, 2), (0, 0))), 1)
        blurred = jnp.where(inside, blurred, 0.0)
        grad_z = (blurred[2:, :, 1:-1] - blurred[:-2, :, 1:-1]) * 0.5
        grad_y = (blurred[1:-1, :, 2:] - blurred[1:-1, :, :-2]) * 0.5
        widened = jnp.pad(blurred[1:-1, :, 1:-1], ((0, 0), (1, 1), (0, 0)))
        grad_x = (widened[:, 2:] - widened[:, :-2]) * 0.5
        square = grad_x * grad_x + grad_y * grad_y + grad_z * grad_z
        diffusivity = 1.0 / (1.0 + square / contrast_squared)
        center = diffusivity[1:-1, :, 1:-1]
        face_x = jnp.concatenate(
            [(center[:, :-1] + center[:, 1:]) * half_scale, jnp.zeros_like(center[:, :1])], 1
        )
        face_y = jnp.where(
            own_y[None, None, :], (center + diffusivity[1:-1, :, 2:]) * half_scale, 0.0
        )
        face_z = jnp.where(
            own_z[:, None, None], (center + diffusivity[2:, :, 1:-1]) * half_scale, 0.0
        )
        solved_x = line_solve(face_x, current, 1)
        lined_y = line_solve(
            lax.all_to_all(face_y, "gy", split_axis=1, concat_axis=2, tiled=True),
            lax.all_to_all(current, "gy", split_axis=1, concat_axis=2, tiled=True),
            2,
        )
        solved_y = lax.all_to_all(lined_y, "gy", split_axis=2, concat_axis=1, tiled=True)
        lined_z = line_solve(
            lax.all_to_all(face_z, "gz", split_axis=1, concat_axis=0, tiled=True),
            lax.all_to_all(current, "gz", split_axis=1, concat_axis=0, tiled=True),
            0,
        )
        solved_z = lax.all_to_all(lined_z, "gz", split_axis=0, concat_axis=1, tiled=True)
        current = (solved_x + solved_y + solved_z) / 3.0
    return current


def solution(mesh):
    in_specs = (P("gz", None, "gy"), P())
    out_specs = P("gz", None, "gy")
    return jax.shard_map(
        on_device, mesh=mesh, in_specs=in_specs, out_specs=out_specs, check_vma=False
    )
```

profile of v0, /device:TPU:2, one launch (start us, length us, event | category | flops | bytes accessed | tf_op | source)
XLA Modules:
  0.0 528.9 jit_solution(7200915971150292406)
XLA Ops:
  12.6 7.8 %collective-permute-done = f32[16,128,4]{1,0,2:T(8,128)S(1)} collective-permute-done((f32[16,128,4]{1,0,2:T(8,128)S(1)}, f32[16,128,4]{1,0,2:T(8,128)S(1)}, u32[]{:S(2)}, u32[]{:S(2)}) %collective-permute-start) | collective-permute-done | bytes 32800 | tf_op jit(solution)/shard_map/ppermute | solution.py:16
  30.3 9.2 %collective-permute-done.2 = f32[4,128,136]{2,0,1:T(4,128)S(1)} collective-permute-done((f32[4,128,136]{2,0,1:T(4,128)S(1)}, f32[4,128,136]{2,0,1:T(4,128)S(1)}, u32[]{:S(2)}, u32[]{:S(2)}) %collective-permute-start.2) | collective-permute-done | bytes 278560 | tf_op jit(solution)/shard_map/ppermute | solution.py:16
  46.3 4.7 fusion.53
  72.9 6.2 %copy.1330 = f32[16,16,8,128]{1,0,3,2:T(8,128)} copy(f32[16,16,8,128]{3,0,1,2:T(8,128)} %bitcast.28) | data formatting | bytes 2097152 | tf_op jit(solution)/shard_map/all_to_all | solution.py:126
  79.1 4.6 slice.2057
  85.8 4.3 all-to-all-start.3
  90.1 5.1 copy.1331
  95.2 7.2 %slice.2599 = f32[16,16,1023]{1,0,2:T(8,128)} slice(f32[16,16,1024]{1,0,2:T(8,128)} %bitcast.296), slice={[0:16], [0:16], [0:1023]} | slice | bytes 2095104 | tf_op jit(solution)/shard_map/slice | solution.py:25
  102.4 11.4 %bitcast_negate_fusion.3 = (f32[16,16,1024]{1,0,2:T(8,128)}, f32[16,16,1024]{1,0,2:T(8,128)S(1)}, f32[16,16,1024]{1,0,2:T(8,128)}) fusion(f32[16,16,8,128]{1,0,3,2:T(8,128)} %copy.1331, f32[16,16,1023]{1,0,2:T(8,128)} %slice.2599), kind=kLoop, calls=%fused_computation.938 | loop fusion | flops 1048576 | bytes 5241856 | tf_op jit(solution)/shard_map/neg | solution.py:73
  116.3 5.3 copy-done.1
  124.2 20.4 %fusion.2 = (f32[16,16,512]{1,0,2:T(8,128)}, f32[16,16,512]{1,0,2:T(8,128)}, f32[16,16,512]{1,0,2:T(8,128)}, f32[16,16,512]{1,0,2:T(8,128)}) fusion(f32[16,16,512]{1,0,2:T(8,128)} %slice.2057, f32[16,16,1024]{1,0,2:T(8,128)} %bitcast.299, f32[16,16,1024]{1,0,2:T(8,128)S(1)} %get-tuple-element.34, f32[16,16,1024]{1,0,2:T(8,128)} %get-tuple-element.35, ...), kind=kLoop, calls=%fused_computation.18 | loop fusion | flops 1835008 | bytes 7340032 | tf_op jit(solution)/shard_map/add | solution.py:52
  144.6 5.3 fusion.5
  156.2 6.8 %fusion.60 = (f32[16,16,256]{1,0,2:T(8,128)}, f32[16,16,256]{1,0,2:T(8,128)S(1)}, f32[16,16,256]{1,0,2:T(8,128)S(1)}, f32[16,16,256]{1,0,2:T(8,128)}) fusion(f32[16,16,256]{1,0,2:T(8,128)} %slice.2068, f32[16,16,512]{1,0,2:T(8,128)S(1)} %copy-done.8, f32[16,16,512]{1,0,2:T(8,128)S(1)} %copy-done.4, f32[16,16,512]{1,0,2:T(8,128)S(1)} %copy-done.5, ...), kind=kLoop, calls=%fused_computation.120 | loop fusion | flops 917504 | bytes 3670016 | tf_op jit(solution)/shard_map/add | solution.py:52
  170.5 5.7 %fusion.82 = (f32[16,16,128]{1,0,2:T(8,128)}, f32[16,16,128]{1,0,2:T(8,128)S(1)}, f32[16,16,128]{1,0,2:T(8,128)}, f32[16,16,128]{1,0,2:T(8,128)}) fusion(f32[16,16,128]{1,0,2:T(8,128)} %slice.2080, f32[16,16,256]{1,0,2:T(8,128)} %get-tuple-element.25, f32[16,16,256]{1,0,2:T(8,128)S(1)} %get-tuple-element.26, f32[16,16,256]{1,0,2:T(8,128)S(1)} %get-tuple-element.31, ...), kind=kLoop, calls=%fused_computation.156 | loop fusion | flops 458752 | bytes 1835008 | tf_op jit(solution)/shard_map/add | solution.py:52
  186.6 5.0 all-to-all-start.4
  196.1 5.9 %fusion.10 = f32[16,16,512,1]{1,0,2,3:T(8,128)S(1)} fusion(f32[16,16,512]{1,0,2:T(8,128)S(1)} %bitcast.304, f32[16,16,1024]{1,0,2:T(8,128)} %bitcast.300, f32[16,16,1024]{1,0,2:T(8,128)} %get-tuple-element.33, f32[16,16,1024]{1,0,2:T(8,128)S(1)} %bitcast.293, f32[16,16,1024]{1,0,2:T(8,128)} %get-tuple-element.35), kind=kLoop, calls=%fused_computation.26 | loop fusion | flops 655360 | bytes 3145728 | tf_op jit(solution)/shard_map/stack | solution.py:61
  202.6 4.7 copy.1259
  207.3 8.1 %reshape.239 = f32[8,1,32768]{2,1,0:T(1,128)} reshape(f32[1024,16,16]{2,1,0:T(8,128)} %bitcast.310) | data formatting | bytes 2097152
  217.8 5.6 %all-to-all-start.2 = ((f32[8,1,32768]{2,1,0:T(1,128)}), f32[8,1,32768]{2,1,0:T(1,128)}, u32[]{:S(2)}, u32[]{:S(2)}) async-start(f32[8,1,32768]{2,1,0:T(1,128)} %reshape.239), calls=%async_computation.2 | async-start | bytes 2097152 | tf_op jit(solution)/shard_map/all_to_all | solution.py:129
  229.8 7.6 %all-to-all-done.2 = f32[8,1,32768]{2,1,0:T(1,128)} async-done(((f32[8,1,32768]{2,1,0:T(1,128)}), f32[8,1,32768]{2,1,0:T(1,128)}, u32[]{:S(2)}, u32[]{:S(2)}) %all-to-all-start.2) | async-done | bytes 1048608 | tf_op jit(solution)/shard_map/all_to_all | solution.py:129
  237.4 5.5 %all-to-all-start.5 = ((f32[64,32,128]{2,1,0:T(8,128)}), f32[64,32,128]{2,1,0:T(8,128)S(1)}, u32[]{:S(2)}, u32[]{:S(2)}) async-start(f32[64,32,128]{2,1,0:T(8,128)} %bitcast.92), calls=%async_computation.5 | async-start | bytes 2097152 | tf_op jit(solution)/shard_map/all_to_all | solution.py:135
  251.9 6.2 %reshape.240 = f32[1024,16,16]{2,1,0:T(8,128)} reshape(f32[8,32768]{1,0:T(8,128)S(1)} %reduce) | data formatting | bytes 2097152
  258.1 5.7 %copy.1261 = f32[16,8,16,128]{3,0,2,1:T(8,128)S(1)} copy(f32[16,8,16,128]{2,0,3,1:T(8,128)} %bitcast.308) | data formatting | bytes 2097152 | tf_op jit(solution)/shard_map/all_to_all | solution.py:129
  263.8 5.1 all-to-all-done.5
  286.8 4.4 all-to-all-start.6
  292.3 5.3 %collective-permute-done.6 = f32[4,128,136]{2,0,1:T(4,128)S(1)} collective-permute-done((f32[4,128,136]{2,0,1:T(4,128)}, f32[4,128,136]{2,0,1:T(4,128)S(1)}, u32[]{:S(2)}, u32[]{:S(2)}) %collective-permute-start.6) | collective-permute-done | bytes 278560 | tf_op jit(solution)/shard_map/ppermute | solution.py:16
  304.3 4.7 fusion.36
  330.6 6.2 %copy.1337 = f32[16,16,8,128]{1,0,3,2:T(8,128)} copy(f32[16,16,8,128]{3,0,1,2:T(8,128)} %bitcast.124) | data formatting | bytes 2097152 | tf_op jit(solution)/shard_map/all_to_all | solution.py:126
  336.8 4.6 slice.2371
  347.8 5.1 copy.1338
  352.9 7.2 %slice.2645 = f32[16,16,1023]{1,0,2:T(8,128)} slice(f32[16,16,1024]{1,0,2:T(8,128)} %bitcast.297), slice={[0:16], [0:16], [0:1023]} | slice | bytes 2095104 | tf_op jit(solution)/shard_map/slice | solution.py:25
  360.2 11.4 %bitcast_negate_fusion.1 = (f32[16,16,1024]{1,0,2:T(8,128)}, f32[16,16,1024]{1,0,2:T(8,128)S(1)}, f32[16,16,1024]{1,0,2:T(8,128)}) fusion(f32[16,16,8,128]{1,0,3,2:T(8,128)} %copy.1338, f32[16,16,1023]{1,0,2:T(8,128)} %slice.2645), kind=kLoop, calls=%fused_computation.936 | loop fusion | flops 1048576 | bytes 5241856 | tf_op jit(solution)/shard_map/neg | solution.py:73
  374.1 5.3 copy-done.3
  381.9 20.4 %fusion.13 = (f32[16,16,512]{1,0,2:T(8,128)}, f32[16,16,512]{1,0,2:T(8,128)}, f32[16,16,512]{1,0,2:T(8,128)}, f32[16,16,512]{1,0,2:T(8,128)}) fusion(f32[16,16,512]{1,0,2:T(8,128)} %slice.2371, f32[16,16,1024]{1,0,2:T(8,128)} %bitcast.302, f32[16,16,1024]{1,0,2:T(8,128)S(1)} %get-tuple-element.30, f32[16,16,1024]{1,0,2:T(8,128)} %get-tuple-element.36, ...), kind=kLoop, calls=%fused_computation.29 | loop fusion | flops 1835008 | bytes 7340032 | tf_op jit(solution)/shard_map/add | solution.py:52
  402.4 5.3 fusion.16
  413.9 7.0 %fusion.71 = (f32[16,16,256]{1,0,2:T(8,128)}, f32[16,16,256]{1,0,2:T(8,128)S(1)}, f32[16,16,256]{1,0,2:T(8,128)S(1)}, f32[16,16,256]{1,0,2:T(8,128)}) fusion(f32[16,16,256]{1,0,2:T(8,128)} %slice.2382, f32[16,16,512]{1,0,2:T(8,128)S(1)} %copy-done.9, f32[16,16,512]{1,0,2:T(8,128)S(1)} %copy-done.6, f32[16,16,512]{1,0,2:T(8,128)S(1)} %copy-done.7, ...), kind=kLoop, calls=%fused_computation.131 | loop fusion | flops 917504 | bytes 3670016 | tf_op jit(solution)/shard_map/add | solution.py:52
  428.5 5.7 %fusion.93 = (f32[16,16,128]{1,0,2:T(8,128)}, f32[16,16,128]{1,0,2:T(8,128)S(1)}, f32[16,16,128]{1,0,2:T(8,128)}, f32[16,16,128]{1,0,2:T(8,128)}) fusion(f32[16,16,128]{1,0,2:T(8,128)} %slice.2394, f32[16,16,256]{1,0,2:T(8,128)} %get-tuple-element.23, f32[16,16,256]{1,0,2:T(8,128)S(1)} %get-tuple-element.24, f32[16,16,256]{1,0,2:T(8,128)S(1)} %get-tuple-element.27, ...), kind=kLoop, calls=%fused_computation.167 | loop fusion | flops 458752 | bytes 1835008 | tf_op jit(solution)/shard_map/add | solution.py:52
  444.6 5.0 all-to-all-start.10
  454.1 5.9 %fusion.21 = f32[16,16,512,1]{1,0,2,3:T(8,128)S(1)} fusion(f32[16,16,512]{1,0,2:T(8,128)S(1)} %bitcast.306, f32[16,16,1024]{1,0,2:T(8,128)} %bitcast.303, f32[16,16,1024]{1,0,2:T(8,128)} %get-tuple-element.29, f32[16,16,1024]{1,0,2:T(8,128)S(1)} %bitcast.295, f32[16,16,1024]{1,0,2:T(8,128)} %get-tuple-element.36), kind=kLoop, calls=%fused_computation.37 | loop fusion | flops 655360 | bytes 3145728 | tf_op jit(solution)/shard_map/stack | solution.py:61
  460.5 4.7 copy.1314
  465.2 8.1 %reshape.241 = f32[8,1,32768]{2,1,0:T(1,128)} reshape(f32[1024,16,16]{2,1,0:T(8,128)} %bitcast.311) | data formatting | bytes 2097152
  475.7 5.9 %all-to-all-start.8 = ((f32[8,1,32768]{2,1,0:T(1,128)}), f32[8,1,32768]{2,1,0:T(1,128)}, u32[]{:S(2)}, u32[]{:S(2)}) async-start(f32[8,1,32768]{2,1,0:T(1,128)} %reshape.241), calls=%async_computation.8 | async-start | bytes 2097152 | tf_op jit(solution)/shard_map/all_to_all | solution.py:129
  488.0 7.6 %all-to-all-done.8 = f32[8,1,32768]{2,1,0:T(1,128)} async-done(((f32[8,1,32768]{2,1,0:T(1,128)}), f32[8,1,32768]{2,1,0:T(1,128)}, u32[]{:S(2)}, u32[]{:S(2)}) %all-to-all-start.8) | async-done | bytes 1048608 | tf_op jit(solution)/shard_map/all_to_all | solution.py:129
  495.6 5.1 all-to-all-start.11
  504.9 4.3 reduce.1
  509.2 6.2 %reshape.242 = f32[1024,16,16]{2,1,0:T(8,128)} reshape(f32[8,32768]{1,0:T(8,128)S(1)} %reduce.1) | data formatting | bytes 2097152
  515.3 5.7 %copy.1316 = f32[16,8,16,128]{3,0,2,1:T(8,128)S(1)} copy(f32[16,8,16,128]{2,0,3,1:T(8,128)} %bitcast.309) | data formatting | bytes 2097152 | tf_op jit(solution)/shard_map/all_to_all | solution.py:129
  521.1 5.6 %all-to-all-done.11 = f32[64,32,128]{2,1,0:T(8,128)S(1)} async-done(((f32[64,32,128]{2,1,0:T(8,128)}), f32[64,32,128]{2,1,0:T(8,128)S(1)}, u32[]{:S(2)}, u32[]{:S(2)}) %all-to-all-start.11) | async-done | bytes 1048608 | tf_op jit(solution)/shard_map/all_to_all | solution.py:135
  (549 shorter events, 205.8 us)
Async XLA Ops:
  0.0 7.2 %copy-start.18 = (f32[16,128,128]{2,1,0:T(8,128)S(1)}, f32[16,128,128]{2,1,0:T(8,128)}, u32[]{:S(2)}) copy-start(f32[16,128,128]{2,1,0:T(8,128)} %param.2) | copy-start | bytes 3145732
  2.9 65.2 %all-to-all-start = ((f32[16,128,128]{2,0,1:T(8,128)}), f32[16,128,128]{2,0,1:T(8,128)}, u32[]{:S(2)}, u32[]{:S(2)}) async-start(f32[16,128,128]{2,0,1:T(8,128)} %copy.1217), calls=%async_computation | async-start | bytes 2097152 | tf_op jit(solution)/shard_map/all_to_all | solution.py:126
  7.8 13.1 %collective-permute-start.1 = (f32[16,128,4]{1,0,2:T(8,128)S(1)}, f32[16,128,4]{1,0,2:T(8,128)S(1)}, u32[]{:S(2)}, u32[]{:S(2)}) collective-permute-start(f32[16,128,4]{1,0,2:T(8,128)S(1)} %copy.1344), channel_id=1, source_target_pairs={{4,0},{8,4},{12,8},{16,12},{20,16},{24,20},{28,24},{5,1},{9,5},{13... | collective-permute-start | bytes 98312 | tf_op jit(solution)/shard_map/ppermute | solution.py:19
  10.2 10.2 %collective-permute-start = (f32[16,128,4]{1,0,2:T(8,128)S(1)}, f32[16,128,4]{1,0,2:T(8,128)S(1)}, u32[]{:S(2)}, u32[]{:S(2)}) collective-permute-start(f32[16,128,4]{1,0,2:T(8,128)S(1)} %copy.1343), channel_id=1, source_target_pairs={{0,4},{4,8},{8,12},{12,16},{16,20},{20,24},{24,28},{1,5},{5,9},{9,... | collective-permute-start | bytes 98312 | tf_op jit(solution)/shard_map/ppermute | solution.py:16
  12.5 53.3 %copy-start.69 = (pred[16]{0:T(512)(128)(4,1)}, pred[16]{0:T(512)(128)(4,1)S(1)}, u32[]{:S(2)}) copy-start(pred[16]{0:T(512)(128)(4,1)S(1)} %add_compare_fusion) | copy-start | bytes 52
  12.6 53.3 %copy-start.71 = (pred[128]{0:T(512)(128)(4,1)}, pred[128]{0:T(512)(128)(4,1)S(1)}, u32[]{:S(2)}) copy-start(pred[128]{0:T(512)(128)(4,1)S(1)} %add_compare_fusion.1) | copy-start | bytes 388
  20.9 9.3 %copy-start.75 = (f32[128]{0:T(128)S(1)}, f32[128]{0:T(128)}, u32[]{:S(2)}) copy-start(f32[128]{0:T(128)} %param.3) | copy-start | bytes 1540
  23.6 16.0 %collective-permute-start.2 = (f32[4,128,136]{2,0,1:T(4,128)S(1)}, f32[4,128,136]{2,0,1:T(4,128)S(1)}, u32[]{:S(2)}, u32[]{:S(2)}) collective-permute-start(f32[4,128,136]{2,0,1:T(4,128)S(1)} %get-tuple-element.63), channel_id=1, source_target_pairs={{0,1},{1,2},{2,3},{4,5},{5,6},{6,7},{8,9},{9,10},{10,11},{12,13},{... | collective-permute-start | bytes 835592 | tf_op jit(solution)/shard_map/ppermute | solution.py:16
  27.5 16.2 %collective-permute-start.3 = (f32[4,128,136]{2,0,1:T(4,128)S(1)}, f32[4,128,136]{2,0,1:T(4,128)S(1)}, u32[]{:S(2)}, u32[]{:S(2)}) collective-permute-start(f32[4,128,136]{2,0,1:T(4,128)S(1)} %get-tuple-element.64), channel_id=1, source_target_pairs={{1,0},{2,1},{3,2},{5,4},{6,5},{7,6},{9,8},{10,9},{11,10},{13,12},{... | collective-permute-start | bytes 835592 | tf_op jit(solution)/shard_map/ppermute | solution.py:19
  30.2 27.3 %copy-start.73 = (f32[128]{0:T(128)}, f32[128]{0:T(128)S(1)}, u32[]{:S(2)}) copy-start(f32[128]{0:T(128)S(1)} %mul.1232) | copy-start | bytes 1540
  30.3 24.2 %copy-start.67 = (pred[20,132]{1,0:T(8,128)(4,1)}, pred[20,132]{1,0:T(8,128)(4,1)S(1)}, u32[]{:S(2)}) copy-start(pred[20,132]{1,0:T(8,128)(4,1)S(1)} %broadcast_and_fusion) | copy-start | bytes 7924
  68.1 17.7 %all-to-all-start.1 = ((f32[16,128,128]{2,0,1:T(8,128)}), f32[16,128,128]{2,0,1:T(8,128)S(1)}, u32[]{:S(2)}, u32[]{:S(2)}) async-start(f32[16,128,128]{2,0,1:T(8,128)} %get-tuple-element.61), calls=%async_computation.1 | async-start | bytes 2097152 | tf_op jit(solution)/shard_map/all_to_all | solution.py:125
  85.8 100.8 %all-to-all-start.3 = ((f32[16,128,128]{2,0,1:T(8,128)}), f32[16,128,128]{2,0,1:T(8,128)}, u32[]{:S(2)}, u32[]{:S(2)}) async-start(f32[16,128,128]{2,0,1:T(8,128)} %copy.1217), calls=%async_computation.3 | async-start | bytes 2097152 | tf_op jit(solution)/shard_map/all_to_all | solution.py:132
  113.8 10.4 %copy-start = (f32[16,16,1024]{1,0,2:T(8,128)}, f32[16,16,1024]{1,0,2:T(8,128)S(1)}, u32[]{:S(2)}) copy-start(f32[16,16,1024]{1,0,2:T(8,128)S(1)} %get-tuple-element.34) | copy-start | bytes 3145732
  113.8 7.8 %copy-start.1 = (f32[16,16,1024]{1,0,2:T(8,128)S(1)}, f32[16,16,1024]{1,0,2:T(8,128)}, u32[]{:S(2)}) copy-start(f32[16,16,1024]{1,0,2:T(8,128)} %get-tuple-element.35) | copy-start | bytes 3145732
  144.6 5.9 %copy-start.4 = (f32[16,16,512]{1,0,2:T(8,128)S(1)}, f32[16,16,512]{1,0,2:T(8,128)}, u32[]{:S(2)}) copy-start(f32[16,16,512]{1,0,2:T(8,128)} %get-tuple-element.20) | copy-start | bytes 1572868
  149.9 3.1 copy-start.8
  163.0 5.3 %copy-start.12 = (f32[16,16,256]{1,0,2:T(8,128)S(1)}, f32[16,16,256]{1,0,2:T(8,128)}, u32[]{:S(2)}) copy-start(f32[16,16,256]{1,0,2:T(8,128)} %get-tuple-element.25) | copy-start | bytes 786436
  186.6 31.2 %all-to-all-start.4 = ((f32[16,128,128]{2,0,1:T(8,128)}), f32[16,128,128]{2,0,1:T(8,128)}, u32[]{:S(2)}, u32[]{:S(2)}) async-start(f32[16,128,128]{2,0,1:T(8,128)} %get-tuple-element.62), calls=%async_computation.4 | async-start | bytes 2097152 | tf_op jit(solution)/shard_map/all_to_all | solution.py:131
  191.7 2.8 slice-start
  217.8 19.7 %all-to-all-start.2 = ((f32[8,1,32768]{2,1,0:T(1,128)}), f32[8,1,32768]{2,1,0:T(1,128)}, u32[]{:S(2)}, u32[]{:S(2)}) async-start(f32[8,1,32768]{2,1,0:T(1,128)} %reshape.239), calls=%async_computation.2 | async-start | bytes 2097152 | tf_op jit(solution)/shard_map/all_to_all | solution.py:129
  228.6 14.4 %copy-start.65 = (f32[16,4,1,128]{3,0,1,2:T(8,128)S(1)}, f32[16,4,1,128]{3,0,1,2:T(8,128)}, u32[]{:S(2)}) copy-start(f32[16,4,1,128]{3,0,1,2:T(8,128)} %fusion.388) | copy-start | bytes 98308
  228.7 15.5 %copy-start.49 = (f32[16,32,128]{2,0,1:T(8,128)S(1)}, f32[16,32,128]{2,0,1:T(8,128)}, u32[]{:S(2)}) copy-start(f32[16,32,128]{2,0,1:T(8,128)} %copy-done.48) | copy-start | bytes 786436
  228.7 16.6 %copy-start.36 = (f32[16,64,128]{2,0,1:T(8,128)S(1)}, f32[16,64,128]{2,0,1:T(8,128)}, u32[]{:S(2)}) copy-start(f32[16,64,128]{2,0,1:T(8,128)} %copy-done.35) | copy-start | bytes 1572868
  228.7 16.6 %copy-start.40 = (f32[16,64,128]{2,0,1:T(8,128)S(1)}, f32[16,64,128]{2,0,1:T(8,128)}, u32[]{:S(2)}) copy-start(f32[16,64,128]{2,0,1:T(8,128)} %copy-done.39) | copy-start | bytes 1572868
  229.8 15.6 %copy-start.44 = (f32[16,64,128]{2,0,1:T(8,128)S(1)}, f32[16,64,128]{2,0,1:T(8,128)}, u32[]{:S(2)}) copy-start(f32[16,64,128]{2,0,1:T(8,128)} %copy-done.43) | copy-start | bytes 1572868
  237.4 31.4 %all-to-all-start.5 = ((f32[64,32,128]{2,1,0:T(8,128)}), f32[64,32,128]{2,1,0:T(8,128)S(1)}, u32[]{:S(2)}, u32[]{:S(2)}) async-start(f32[64,32,128]{2,1,0:T(8,128)} %bitcast.92), calls=%async_computation.5 | async-start | bytes 2097152 | tf_op jit(solution)/shard_map/all_to_all | solution.py:135
  273.0 6.0 %collective-permute-start.4 = (f32[16,128,4]{1,0,2:T(8,128)S(1)}, f32[16,128,4]{1,0,2:T(8,128)S(1)}, u32[]{:S(2)}, u32[]{:S(2)}) collective-permute-start(f32[16,128,4]{1,0,2:T(8,128)S(1)} %copy.1276), channel_id=1, source_target_pairs={{0,4},{4,8},{8,12},{12,16},{16,20},{20,24},{24,28},{1,5},{5,9},{9,... | collective-permute-start | bytes 98312 | tf_op jit(solution)/shard_map/ppermute | solution.py:16
  275.4 5.2 collective-permute-start.5
  284.2 13.4 %collective-permute-start.6 = (f32[4,128,136]{2,0,1:T(4,128)}, f32[4,128,136]{2,0,1:T(4,128)S(1)}, u32[]{:S(2)}, u32[]{:S(2)}) collective-permute-start(f32[4,128,136]{2,0,1:T(4,128)} %get-tuple-element.59), channel_id=1, source_target_pairs={{0,1},{1,2},{2,3},{4,5},{5,6},{6,7},{8,9},{9,10},{10,11},{12,13},{... | collective-permute-start | bytes 835592 | tf_op jit(solution)/shard_map/ppermute | solution.py:16
  285.5 16.1 %collective-permute-start.7 = (f32[4,128,136]{2,0,1:T(4,128)}, f32[4,128,136]{2,0,1:T(4,128)S(1)}, u32[]{:S(2)}, u32[]{:S(2)}) collective-permute-start(f32[4,128,136]{2,0,1:T(4,128)} %get-tuple-element.60), channel_id=1, source_target_pairs={{1,0},{2,1},{3,2},{5,4},{6,5},{7,6},{9,8},{10,9},{11,10},{13,12},{... | collective-permute-start | bytes 835592 | tf_op jit(solution)/shard_map/ppermute | solution.py:19
  286.8 39.4 %all-to-all-start.6 = ((f32[16,128,128]{2,0,1:T(8,128)}), f32[16,128,128]{2,0,1:T(8,128)}, u32[]{:S(2)}, u32[]{:S(2)}) async-start(f32[16,128,128]{2,0,1:T(8,128)} %fusion.111), calls=%async_computation.6 | async-start | bytes 2097152 | tf_op jit(solution)/shard_map/all_to_all | solution.py:126
  309.0 3.4 copy-start.68
  326.2 17.4 %all-to-all-start.7 = ((f32[16,128,128]{2,0,1:T(8,128)}), f32[16,128,128]{2,0,1:T(8,128)S(1)}, u32[]{:S(2)}, u32[]{:S(2)}) async-start(f32[16,128,128]{2,0,1:T(8,128)} %get-tuple-element.57), calls=%async_computation.7 | async-start | bytes 2097152 | tf_op jit(solution)/shard_map/all_to_all | solution.py:125
  343.6 101.0 %all-to-all-start.9 = ((f32[16,128,128]{2,0,1:T(8,128)}), f32[16,128,128]{2,0,1:T(8,128)}, u32[]{:S(2)}, u32[]{:S(2)}) async-start(f32[16,128,128]{2,0,1:T(8,128)} %fusion.111), calls=%async_computation.9 | async-start | bytes 2097152 | tf_op jit(solution)/shard_map/all_to_all | solution.py:132
  371.5 10.4 %copy-start.2 = (f32[16,16,1024]{1,0,2:T(8,128)}, f32[16,16,1024]{1,0,2:T(8,128)S(1)}, u32[]{:S(2)}) copy-start(f32[16,16,1024]{1,0,2:T(8,128)S(1)} %get-tuple-element.30) | copy-start | bytes 3145732
  371.5 7.8 %copy-start.3 = (f32[16,16,1024]{1,0,2:T(8,128)S(1)}, f32[16,16,1024]{1,0,2:T(8,128)}, u32[]{:S(2)}) copy-start(f32[16,16,1024]{1,0,2:T(8,128)} %get-tuple-element.36) | copy-start | bytes 3145732
  402.3 5.9 %copy-start.6 = (f32[16,16,512]{1,0,2:T(8,128)S(1)}, f32[16,16,512]{1,0,2:T(8,128)}, u32[]{:S(2)}) copy-start(f32[16,16,512]{1,0,2:T(8,128)} %get-tuple-element.18) | copy-start | bytes 1572868
  407.6 3.1 copy-start.9
  421.0 5.3 %copy-start.14 = (f32[16,16,256]{1,0,2:T(8,128)S(1)}, f32[16,16,256]{1,0,2:T(8,128)}, u32[]{:S(2)}) copy-start(f32[16,16,256]{1,0,2:T(8,128)} %get-tuple-element.23) | copy-start | bytes 786436
  444.6 31.2 %all-to-all-start.10 = ((f32[16,128,128]{2,0,1:T(8,128)}), f32[16,128,128]{2,0,1:T(8,128)}, u32[]{:S(2)}, u32[]{:S(2)}) async-start(f32[16,128,128]{2,0,1:T(8,128)} %get-tuple-element.58), calls=%async_computation.10 | async-start | bytes 2097152 | tf_op jit(solution)/shard_map/all_to_all | solution.py:131
  475.7 19.8 %all-to-all-start.8 = ((f32[8,1,32768]{2,1,0:T(1,128)}), f32[8,1,32768]{2,1,0:T(1,128)}, u32[]{:S(2)}, u32[]{:S(2)}) async-start(f32[8,1,32768]{2,1,0:T(1,128)} %reshape.241), calls=%async_computation.8 | async-start | bytes 2097152 | tf_op jit(solution)/shard_map/all_to_all | solution.py:129
  486.8 13.9 %copy-start.66 = (f32[16,4,1,128]{3,0,1,2:T(8,128)S(1)}, f32[16,4,1,128]{3,0,1,2:T(8,128)}, u32[]{:S(2)}) copy-start(f32[16,4,1,128]{3,0,1,2:T(8,128)} %fusion.410) | copy-start | bytes 98308
  486.9 15.0 %copy-start.46 = (f32[16,32,128]{2,0,1:T(8,128)S(1)}, f32[16,32,128]{2,0,1:T(8,128)}, u32[]{:S(2)}) copy-start(f32[16,32,128]{2,0,1:T(8,128)} %copy-done.45) | copy-start | bytes 786436
  486.9 16.1 %copy-start.34 = (f32[16,64,128]{2,0,1:T(8,128)S(1)}, f32[16,64,128]{2,0,1:T(8,128)}, u32[]{:S(2)}) copy-start(f32[16,64,128]{2,0,1:T(8,128)} %copy-done.33) | copy-start | bytes 1572868
  486.9 16.1 %copy-start.38 = (f32[16,64,128]{2,0,1:T(8,128)S(1)}, f32[16,64,128]{2,0,1:T(8,128)}, u32[]{:S(2)}) copy-start(f32[16,64,128]{2,0,1:T(8,128)} %copy-done.37) | copy-start | bytes 1572868
  488.0 15.1 %copy-start.42 = (f32[16,64,128]{2,0,1:T(8,128)S(1)}, f32[16,64,128]{2,0,1:T(8,128)}, u32[]{:S(2)}) copy-start(f32[16,64,128]{2,0,1:T(8,128)} %copy-done.41) | copy-start | bytes 1572868
  495.6 31.0 %all-to-all-start.11 = ((f32[64,32,128]{2,1,0:T(8,128)}), f32[64,32,128]{2,1,0:T(8,128)S(1)}, u32[]{:S(2)}, u32[]{:S(2)}) async-start(f32[64,32,128]{2,1,0:T(8,128)} %bitcast.188), calls=%async_computation.11 | async-start | bytes 2097152 | tf_op jit(solution)/shard_map/all_to_all | solution.py:135
  (52 other events, 80.6 us)
where the time goes:
time: 535 us; the launch traced here: 529 us
  other arithmetic  213 us (40%)
  local copies, waits for them, and re-layouts  176 us (33%)
  starting transfers between devices  75.1 us (14%)
  waiting for transfers between devices  61.7 us (12%)
    add x40, other arithmetic, reduce_solve(): new_right = odds[3] + factor_before * before[3] + factor_after * after[3]  74.7 us
    unnamed x167, local copies, waits for them, and re-layouts  56.3 us
    slice x124, local copies, waits for them, and re-layouts, slice_axis(): lax.slice_in_dim(array, start, start + stride * (count - 1) + 1, stride,...  55.3 us
    another operation x86, other arithmetic, reduce_solve(): paired = jnp.stack([solved_even, odd_full], axis=axis + 1)  35.7 us
    mul x40, other arithmetic, reduce_solve(): new_upper = factor_after * after[2]  25 us
    neg x6, other arithmetic, line_solve(): return reduce_solve(-lower, diagonal, -upper, right, axis)  24 us
    ppermute x4, waiting for transfers between devices, extended(): lax.ppermute(lax.slice_in_dim(block, block.shape[dim] - width, None, axis...  22.3 us
    add x4, other arithmetic, smooth_axis(): total + kernel_taps[offset] * slice_axis(padded, offset, count, axis)  16.2 us
  transfers between devices with their start and end apart: 20, of which 12 were waited for; matrix products, arithmetic and copies ran while one was open for 67% of the time, Pallas kernels for 0%

commit v1 on v0

--- a/solution.py
+++ b/solution.py
@@ -6,6 +6,28 @@
 STEPS = 2
 kernel_taps = (0.05448868, 0.24420134, 0.40261995, 0.24420134, 0.05448868)
 half_scale = 600.0
+
+
+def in_blocks(x, dim, peers):
+    before, after = (x.shape[:dim], x.shape[dim + 1 :])
+    return jnp.moveaxis(x.reshape(*before, peers, -1, *after), dim, 0)
+
+
+def in_order(pieces, dim):
+    pieces = jnp.moveaxis(pieces, 0, dim)
+    shape = pieces.shape
+    return pieces.reshape(*shape[:dim], shape[dim] * shape[dim + 1], *shape[dim + 2 :])
+
+
+def swapped_with_each(x, axis, split_dim, concat_dim):
+    size, place = (lax.axis_size(axis), lax.axis_index(axis))
+    pieces = in_blocks(x, split_dim, size)
+    outs = [pieces[place]]
+    for step in range(1, size):
+        sent = pieces[place ^ step]
+        outs.append(lax.ppermute(sent, axis, [(i, i ^ step) for i in range(size)]))
+    pieces = jnp.stack(outs)[place ^ jnp.arange(size)]
+    return in_order(pieces, concat_dim)
 
 
 def extended(block, sides, width):
@@ -128,7 +150,7 @@
         )
         solved_y = lax.all_to_all(lined_y, "gy", split_axis=2, concat_axis=1, tiled=True)
         lined_z = line_solve(
-            lax.all_to_all(face_z, "gz", split_axis=1, concat_axis=0, tiled=True),
+            swapped_with_each(face_z, "gz", 1, 0),
             lax.all_to_all(current, "gz", split_axis=1, concat_axis=0, tiled=True),
             0,
         )

time: 535 us -> 579 us (1.082)
  other arithmetic: 213 us -> 235 us
  waiting for transfers between devices: 61.7 us -> 75.1 us
  local copies, waits for them, and re-layouts: 176 us -> 187 us
    ppermute x0 -> x6, waiting for transfers between devices: none -> 24.4 us  [swapped_with_each(): outs.append(lax.ppermute(sent, axis, [(i, i ^ step) for i in range(size)]))]
    all_to_all x2 -> x0, starting transfers between devices: 10.1 us -> none  [on_device(): lax.all_to_all(face_z, 'gz', split_axis=1, concat_axis=0, tiled=True)]
    ppermute x0 -> x6, starting transfers between devices: none -> 8.77 us  [swapped_with_each(): outs.append(lax.ppermute(sent, axis, [(i, i ^ step) for i in range(size)]))]
    unnamed x167 -> x203, local copies, waits for them, and re-layouts: 56.3 us -> 63.2 us
  transfers between devices with their start and end apart: 20 -> 24, of which waited for: 12 -> 14; matrix products, arithmetic and copies ran while one was open for 67% -> 67% of each run, Pallas kernels for 0% -> 0%
where the time goes in v1:
time: 579 us; the launch traced here: 573 us
  other arithmetic  235 us (41%)
  local copies, waits for them, and re-layouts  187 us (32%)
  waiting for transfers between devices  75.1 us (13%)
  starting transfers between devices  72.5 us (13%)
    add x40, other arithmetic, reduce_solve(): new_right = odds[3] + factor_before * before[3] + factor_after * after[3]  79.1 us
    unnamed x203, local copies, waits for them, and re-layouts  63.2 us
    slice x124, local copies, waits for them, and re-layouts, slice_axis(): lax.slice_in_dim(array, start, start + stride * (count - 1) + 1, stride,...  57.3 us
    another operation x86, other arithmetic, reduce_solve(): paired = jnp.stack([solved_even, odd_full], axis=axis + 1)  38.7 us
    mul x40, other arithmetic, reduce_solve(): new_upper = factor_after * after[2]  30.3 us
    neg x6, other arithmetic, line_solve(): return reduce_solve(-lower, diagonal, -upper, right, axis)  25.9 us
    ppermute x6, waiting for transfers between devices, swapped_with_each(): outs.append(lax.ppermute(sent, axis, [(i, i ^ step) for i in range(size)]))  24.4 us
    ppermute x4, waiting for transfers between devices, extended(): lax.ppermute(lax.slice_in_dim(block, block.shape[dim] - width, None, axis...  17.2 us
  transfers between devices with their start and end apart: 24, of which 14 were waited for; matrix products, arithmetic and copies ran while one was open for 67% of the time, Pallas kernels for 0%

profile of v1, /device:TPU:2, one launch (start us, length us, event | category | flops | bytes accessed | tf_op | source)
XLA Modules:
  0.0 573.1 jit_solution(17970712836092465713)
XLA Ops:
  14.8 5.6 collective-permute-done
  24.5 4.3 collective-permute-start.2
  32.3 8.1 %collective-permute-done.2 = f32[4,128,136]{2,0,1:T(4,128)} collective-permute-done((f32[4,128,136]{2,0,1:T(4,128)}, f32[4,128,136]{2,0,1:T(4,128)}, u32[]{:S(2)}, u32[]{:S(2)}) %collective-permute-start.2) | collective-permute-done | bytes 278560 | tf_op jit(solution)/shard_map/ppermute | solution.py:38
  40.4 4.9 collective-permute-done.3
  48.2 4.6 fusion.53
  83.0 9.8 %collective-permute-done.5 = f32[16,32,128]{2,1,0:T(8,128)} collective-permute-done((f32[16,32,128]{2,1,0:T(8,128)}, f32[16,32,128]{2,1,0:T(8,128)}, u32[]{:S(2)}, u32[]{:S(2)}) %collective-permute-start.5) | collective-permute-done | bytes 262176 | tf_op jit(solution)/shard_map/ppermute | solution.py:28
  100.9 5.0 copy.1376
  105.9 4.5 slice.2057
  114.7 5.0 copy.1377
  119.8 7.2 %slice.2603 = f32[16,16,1023]{1,0,2:T(8,128)} slice(f32[16,16,1024]{1,0,2:T(8,128)} %bitcast.324), slice={[0:16], [0:16], [0:1023]} | slice | bytes 2095104 | tf_op jit(solution)/shard_map/slice | solution.py:47
  127.0 11.4 %bitcast_negate_fusion.3 = (f32[16,16,1024]{1,0,2:T(8,128)}, f32[16,16,1024]{1,0,2:T(8,128)S(1)}, f32[16,16,1024]{1,0,2:T(8,128)}) fusion(f32[16,16,8,128]{1,0,3,2:T(8,128)} %copy.1377, f32[16,16,1023]{1,0,2:T(8,128)} %slice.2603), kind=kLoop, calls=%fused_computation.961 | loop fusion | flops 1048576 | bytes 5241856 | tf_op jit(solution)/shard_map/neg | solution.py:95
  145.7 20.0 %fusion.2 = (f32[16,16,512]{1,0,2:T(8,128)}, f32[16,16,512]{1,0,2:T(8,128)}, f32[16,16,512]{1,0,2:T(8,128)}, f32[16,16,512]{1,0,2:T(8,128)}) fusion(f32[16,16,512]{1,0,2:T(8,128)} %slice.2057, f32[16,16,1024]{1,0,2:T(8,128)} %bitcast.327, f32[16,16,1024]{1,0,2:T(8,128)S(1)} %get-tuple-element.34, f32[16,16,1024]{1,0,2:T(8,128)} %get-tuple-element.35, ...), kind=kLoop, calls=%fused_computation.20 | loop fusion | flops 1835008 | bytes 7340032 | tf_op jit(solution)/shard_map/add | solution.py:74
  165.7 7.4 %fusion.5 = f32[16,16,512]{1,0,2:T(8,128)} fusion(f32[16,16,512]{1,0,2:T(8,128)} %get-tuple-element.32, f32[16,16,512]{1,0,2:T(8,128)} %slice.2064, f32[16,16,1024]{1,0,2:T(8,128)} %get-tuple-element.33), kind=kLoop, calls=%fused_computation.23 | loop fusion | flops 393216 | bytes 2097152 | tf_op jit(solution)/shard_map/mul | solution.py:73
  179.2 9.3 %fusion.60 = (f32[16,16,256]{1,0,2:T(8,128)}, f32[16,16,256]{1,0,2:T(8,128)S(1)}, f32[16,16,256]{1,0,2:T(8,128)S(1)}, f32[16,16,256]{1,0,2:T(8,128)}) fusion(f32[16,16,256]{1,0,2:T(8,128)} %slice.2068, f32[16,16,512]{1,0,2:T(8,128)} %get-tuple-element.19, f32[16,16,512]{1,0,2:T(8,128)S(1)} %copy-done.2, f32[16,16,512]{1,0,2:T(8,128)S(1)} %copy-done.3, ...), kind=kLoop, calls=%fused_computation.122 | loop fusion | flops 917504 | bytes 3670016 | tf_op jit(solution)/shard_map/add | solution.py:74
  188.5 4.8 fusion.63
  196.6 6.2 %fusion.82 = (f32[16,16,128]{1,0,2:T(8,128)}, f32[16,16,128]{1,0,2:T(8,128)}, f32[16,16,128]{1,0,2:T(8,128)}, f32[16,16,128]{1,0,2:T(8,128)}) fusion(f32[16,16,128]{1,0,2:T(8,128)} %slice.2080, f32[16,16,256]{1,0,2:T(8,128)} %get-tuple-element.25, f32[16,16,256]{1,0,2:T(8,128)S(1)} %get-tuple-element.26, f32[16,16,256]{1,0,2:T(8,128)S(1)} %get-tuple-element.31, ...), kind=kLoop, calls=%fused_computation.158 | loop fusion | flops 458752 | bytes 1835008 | tf_op jit(solution)/shard_map/add | solution.py:74
  219.1 6.2 %fusion.10 = f32[16,16,512,1]{1,0,2,3:T(8,128)} fusion(f32[16,16,512]{1,0,2:T(8,128)S(1)} %bitcast.332, f32[16,16,1024]{1,0,2:T(8,128)} %bitcast.328, f32[16,16,1024]{1,0,2:T(8,128)} %get-tuple-element.33, f32[16,16,1024]{1,0,2:T(8,128)S(1)} %get-tuple-element.34, f32[16,16,1024]{1,0,2:T(8,128)S(1)} %bitcast.321), kind=kLoop, calls=%fused_computation.28 | loop fusion | flops 655360 | bytes 3145728 | tf_op jit(solution)/shard_map/stack | solution.py:83
  228.0 4.7 copy.1299
  232.7 8.1 %reshape.301 = f32[8,1,32768]{2,1,0:T(1,128)} reshape(f32[1024,16,16]{2,1,0:T(8,128)} %bitcast.338) | data formatting | bytes 2097152
  240.9 4.7 all-to-all-start.2
  251.0 7.6 %all-to-all-done.2 = f32[8,1,32768]{2,1,0:T(1,128)} async-done(((f32[8,1,32768]{2,1,0:T(1,128)}), f32[8,1,32768]{2,1,0:T(1,128)}, u32[]{:S(2)}, u32[]{:S(2)}) %all-to-all-start.2) | async-done | bytes 1048608 | tf_op jit(solution)/shard_map/all_to_all | solution.py:151
  258.6 5.0 all-to-all-start.4
  270.1 4.3 reduce
  274.5 6.2 %reshape.302 = f32[1024,16,16]{2,1,0:T(8,128)} reshape(f32[8,32768]{1,0:T(8,128)S(1)} %reduce) | data formatting | bytes 2097152
  280.7 5.7 copy.1301
  309.5 4.9 all-to-all-start.5
  319.0 5.5 collective-permute-done.10
  327.5 4.5 fusion.36
  364.1 9.0 %collective-permute-done.12 = f32[16,32,128]{2,1,0:T(8,128)} collective-permute-done((f32[16,32,128]{2,1,0:T(8,128)}, f32[16,32,128]{2,1,0:T(8,128)}, u32[]{:S(2)}, u32[]{:S(2)}) %collective-permute-start.12) | collective-permute-done | bytes 262176 | tf_op jit(solution)/shard_map/ppermute | solution.py:28
  381.2 5.0 copy.1383
  386.2 4.5 slice.2371
  395.0 5.0 copy.1384
  400.0 7.2 %slice.2649 = f32[16,16,1023]{1,0,2:T(8,128)} slice(f32[16,16,1024]{1,0,2:T(8,128)} %bitcast.325), slice={[0:16], [0:16], [0:1023]} | slice | bytes 2095104 | tf_op jit(solution)/shard_map/slice | solution.py:47
  407.3 11.4 %bitcast_negate_fusion.1 = (f32[16,16,1024]{1,0,2:T(8,128)}, f32[16,16,1024]{1,0,2:T(8,128)S(1)}, f32[16,16,1024]{1,0,2:T(8,128)}) fusion(f32[16,16,8,128]{1,0,3,2:T(8,128)} %copy.1384, f32[16,16,1023]{1,0,2:T(8,128)} %slice.2649), kind=kLoop, calls=%fused_computation.959 | loop fusion | flops 1048576 | bytes 5241856 | tf_op jit(solution)/shard_map/neg | solution.py:95
  426.0 20.0 %fusion.13 = (f32[16,16,512]{1,0,2:T(8,128)}, f32[16,16,512]{1,0,2:T(8,128)}, f32[16,16,512]{1,0,2:T(8,128)}, f32[16,16,512]{1,0,2:T(8,128)}) fusion(f32[16,16,512]{1,0,2:T(8,128)} %slice.2371, f32[16,16,1024]{1,0,2:T(8,128)} %bitcast.330, f32[16,16,1024]{1,0,2:T(8,128)S(1)} %get-tuple-element.30, f32[16,16,1024]{1,0,2:T(8,128)} %get-tuple-element.36, ...), kind=kLoop, calls=%fused_computation.31 | loop fusion | flops 1835008 | bytes 7340032 | tf_op jit(solution)/shard_map/add | solution.py:74
  446.0 7.4 %fusion.16 = f32[16,16,512]{1,0,2:T(8,128)} fusion(f32[16,16,512]{1,0,2:T(8,128)} %get-tuple-element.28, f32[16,16,512]{1,0,2:T(8,128)} %slice.2378, f32[16,16,1024]{1,0,2:T(8,128)} %get-tuple-element.29), kind=kLoop, calls=%fused_computation.34 | loop fusion | flops 393216 | bytes 2097152 | tf_op jit(solution)/shard_map/mul | solution.py:73
  459.5 9.1 %fusion.71 = (f32[16,16,256]{1,0,2:T(8,128)}, f32[16,16,256]{1,0,2:T(8,128)S(1)}, f32[16,16,256]{1,0,2:T(8,128)S(1)}, f32[16,16,256]{1,0,2:T(8,128)}) fusion(f32[16,16,256]{1,0,2:T(8,128)} %slice.2382, f32[16,16,512]{1,0,2:T(8,128)} %get-tuple-element.17, f32[16,16,512]{1,0,2:T(8,128)S(1)} %copy-done.4, f32[16,16,512]{1,0,2:T(8,128)S(1)} %copy-done.5, ...), kind=kLoop, calls=%fused_computation.133 | loop fusion | flops 917504 | bytes 3670016 | tf_op jit(solution)/shard_map/add | solution.py:74
  468.6 4.8 fusion.74
  476.6 6.0 %fusion.93 = (f32[16,16,128]{1,0,2:T(8,128)}, f32[16,16,128]{1,0,2:T(8,128)}, f32[16,16,128]{1,0,2:T(8,128)}, f32[16,16,128]{1,0,2:T(8,128)}) fusion(f32[16,16,128]{1,0,2:T(8,128)} %slice.2394, f32[16,16,256]{1,0,2:T(8,128)} %get-tuple-element.23, f32[16,16,256]{1,0,2:T(8,128)S(1)} %get-tuple-element.24, f32[16,16,256]{1,0,2:T(8,128)S(1)} %get-tuple-element.27, ...), kind=kLoop, calls=%fused_computation.169 | loop fusion | flops 458752 | bytes 1835008 | tf_op jit(solution)/shard_map/add | solution.py:74
  498.9 6.2 %fusion.21 = f32[16,16,512,1]{1,0,2,3:T(8,128)} fusion(f32[16,16,512]{1,0,2:T(8,128)S(1)} %bitcast.334, f32[16,16,1024]{1,0,2:T(8,128)} %bitcast.331, f32[16,16,1024]{1,0,2:T(8,128)} %get-tuple-element.29, f32[16,16,1024]{1,0,2:T(8,128)S(1)} %get-tuple-element.30, f32[16,16,1024]{1,0,2:T(8,128)S(1)} %bitcast.323), kind=kLoop, calls=%fused_computation.39 | loop fusion | flops 655360 | bytes 3145728 | tf_op jit(solution)/shard_map/stack | solution.py:83
  507.8 4.7 copy.1357
  512.5 8.1 %reshape.303 = f32[8,1,32768]{2,1,0:T(1,128)} reshape(f32[1024,16,16]{2,1,0:T(8,128)} %bitcast.339) | data formatting | bytes 2097152
  520.7 4.7 all-to-all-start.7
  530.8 7.6 %all-to-all-done.7 = f32[8,1,32768]{2,1,0:T(1,128)} async-done(((f32[8,1,32768]{2,1,0:T(1,128)}), f32[8,1,32768]{2,1,0:T(1,128)}, u32[]{:S(2)}, u32[]{:S(2)}) %all-to-all-start.7) | async-done | bytes 1048608 | tf_op jit(solution)/shard_map/all_to_all | solution.py:151
  538.4 5.0 all-to-all-start.9
  549.4 4.3 reduce.1
  553.8 6.2 %reshape.304 = f32[1024,16,16]{2,1,0:T(8,128)} reshape(f32[8,32768]{1,0:T(8,128)S(1)} %reduce.1) | data formatting | bytes 2097152
  560.0 5.7 copy.1359
  (599 shorter events, 242.2 us)
Async XLA Ops:
  0.0 7.2 %copy-start.30 = (f32[16,128,128]{2,1,0:T(8,128)S(1)}, f32[16,128,128]{2,1,0:T(8,128)}, u32[]{:S(2)}) copy-start(f32[16,128,128]{2,1,0:T(8,128)} %param.2) | copy-start | bytes 3145732
  2.9 73.6 %all-to-all-start = ((f32[16,128,128]{2,0,1:T(8,128)}), f32[16,128,128]{2,0,1:T(8,128)S(1)}, u32[]{:S(2)}, u32[]{:S(2)}) async-start(f32[16,128,128]{2,0,1:T(8,128)} %copy.1257), calls=%async_computation | async-start | bytes 2097152 | tf_op jit(solution)/shard_map/all_to_all | solution.py:148
  10.0 10.9 %collective-permute-start.1 = (f32[16,128,4]{1,0,2:T(8,128)S(1)}, f32[16,128,4]{1,0,2:T(8,128)S(1)}, u32[]{:S(2)}, u32[]{:S(2)}) collective-permute-start(f32[16,128,4]{1,0,2:T(8,128)S(1)} %copy.1390), channel_id=1, source_target_pairs={{4,0},{8,4},{12,8},{16,12},{20,16},{24,20},{28,24},{5,1},{9,5},{13... | collective-permute-start | bytes 98312 | tf_op jit(solution)/shard_map/ppermute | solution.py:41
  12.4 8.0 %collective-permute-start = (f32[16,128,4]{1,0,2:T(8,128)S(1)}, f32[16,128,4]{1,0,2:T(8,128)S(1)}, u32[]{:S(2)}, u32[]{:S(2)}) collective-permute-start(f32[16,128,4]{1,0,2:T(8,128)S(1)} %copy.1389), channel_id=1, source_target_pairs={{0,4},{4,8},{8,12},{12,16},{16,20},{20,24},{24,28},{1,5},{5,9},{9,... | collective-permute-start | bytes 98312 | tf_op jit(solution)/shard_map/ppermute | solution.py:38
  14.7 48.5 %copy-start.83 = (pred[16]{0:T(512)(128)(4,1)}, pred[16]{0:T(512)(128)(4,1)S(1)}, u32[]{:S(2)}) copy-start(pred[16]{0:T(512)(128)(4,1)S(1)} %add_compare_fusion) | copy-start | bytes 52
  14.8 48.5 %copy-start.85 = (pred[128]{0:T(512)(128)(4,1)}, pred[128]{0:T(512)(128)(4,1)S(1)}, u32[]{:S(2)}) copy-start(pred[128]{0:T(512)(128)(4,1)S(1)} %add_compare_fusion.1) | copy-start | bytes 388
  14.8 80.2 %copy-start.82 = (s32[1024]{0:T(1024)}, s32[1024]{0:T(1024)S(1)}, u32[]{:S(2)}) copy-start(s32[1024]{0:T(1024)S(1)} %pad_clamp_fusion) | copy-start | bytes 12292
  20.9 11.3 %copy-start.89 = (f32[128]{0:T(128)S(1)}, f32[128]{0:T(128)}, u32[]{:S(2)}) copy-start(f32[128]{0:T(128)} %param.3) | copy-start | bytes 1540
  24.5 15.8 %collective-permute-start.2 = (f32[4,128,136]{2,0,1:T(4,128)}, f32[4,128,136]{2,0,1:T(4,128)}, u32[]{:S(2)}, u32[]{:S(2)}) collective-permute-start(f32[4,128,136]{2,0,1:T(4,128)} %get-tuple-element.63), channel_id=1, source_target_pairs={{0,1},{1,2},{2,3},{4,5},{5,6},{6,7},{8,9},{9,10},{10,11},{12,13},{... | collective-permute-start | bytes 835592 | tf_op jit(solution)/shard_map/ppermute | solution.py:38
  28.8 16.5 %collective-permute-start.3 = (f32[4,128,136]{2,0,1:T(4,128)}, f32[4,128,136]{2,0,1:T(4,128)}, u32[]{:S(2)}, u32[]{:S(2)}) collective-permute-start(f32[4,128,136]{2,0,1:T(4,128)} %get-tuple-element.64), channel_id=1, source_target_pairs={{1,0},{2,1},{3,2},{5,4},{6,5},{7,6},{9,8},{10,9},{11,10},{13,12},{... | collective-permute-start | bytes 835592 | tf_op jit(solution)/shard_map/ppermute | solution.py:41
  32.2 27.1 %copy-start.87 = (f32[128]{0:T(128)}, f32[128]{0:T(128)S(1)}, u32[]{:S(2)}) copy-start(f32[128]{0:T(128)S(1)} %mul.1232) | copy-start | bytes 1540
  32.3 23.9 %copy-start.80 = (pred[20,132]{1,0:T(8,128)(4,1)}, pred[20,132]{1,0:T(8,128)(4,1)S(1)}, u32[]{:S(2)}) copy-start(pred[20,132]{1,0:T(8,128)(4,1)S(1)} %broadcast_and_fusion) | copy-start | bytes 7924
  67.6 13.4 %collective-permute-start.6 = (f32[16,32,128]{2,1,0:T(8,128)}, f32[16,32,128]{2,1,0:T(8,128)}, u32[]{:S(2)}, u32[]{:S(2)}) collective-permute-start(f32[16,32,128]{2,1,0:T(8,128)} %bitcast.316), channel_id=1, source_target_pairs={{0,3},{1,2},{2,1},{3,0},{4,7},{5,6},{6,5},{7,4},{8,11},{9,10},{10,... | collective-permute-start | bytes 786440 | tf_op jit(solution)/shard_map/ppermute | solution.py:28
  68.4 14.6 %collective-permute-start.4 = (f32[16,32,128]{2,1,0:T(8,128)}, f32[16,32,128]{2,1,0:T(8,128)}, u32[]{:S(2)}, u32[]{:S(2)}) collective-permute-start(f32[16,32,128]{2,1,0:T(8,128)} %bitcast.318), channel_id=1, source_target_pairs={{0,1},{1,0},{2,3},{3,2},{4,5},{5,4},{6,7},{7,6},{8,9},{9,8},{10,11... | collective-permute-start | bytes 786440 | tf_op jit(solution)/shard_map/ppermute | solution.py:28
  70.0 22.9 %collective-permute-start.5 = (f32[16,32,128]{2,1,0:T(8,128)}, f32[16,32,128]{2,1,0:T(8,128)}, u32[]{:S(2)}, u32[]{:S(2)}) collective-permute-start(f32[16,32,128]{2,1,0:T(8,128)} %bitcast.317), channel_id=1, source_target_pairs={{0,2},{1,3},{2,0},{3,1},{4,6},{5,7},{6,4},{7,5},{8,10},{9,11},{10,... | collective-permute-start | bytes 786440 | tf_op jit(solution)/shard_map/ppermute | solution.py:28
  76.4 34.0 %all-to-all-start.1 = ((f32[16,128,128]{2,0,1:T(8,128)}), f32[16,128,128]{2,0,1:T(8,128)S(1)}, u32[]{:S(2)}, u32[]{:S(2)}) async-start(f32[16,128,128]{2,0,1:T(8,128)} %get-tuple-element.61), calls=%async_computation.1 | async-start | bytes 2097152 | tf_op jit(solution)/shard_map/all_to_all | solution.py:147
  80.3 12.5 %copy-start.79 = (f32[16,2,2,128]{3,0,2,1:T(8,128)}, f32[16,2,2,128]{3,0,2,1:T(8,128)S(1)}, u32[]{:S(2)}) copy-start(f32[16,2,2,128]{3,0,2,1:T(8,128)S(1)} %copy.1264) | copy-start | bytes 98308
  110.4 130.4 %all-to-all-start.3 = ((f32[16,128,128]{2,0,1:T(8,128)}), f32[16,128,128]{2,0,1:T(8,128)}, u32[]{:S(2)}, u32[]{:S(2)}) async-start(f32[16,128,128]{2,0,1:T(8,128)} %copy.1257), calls=%async_computation.3 | async-start | bytes 2097152 | tf_op jit(solution)/shard_map/all_to_all | solution.py:154
  165.7 7.4 %copy-start.2 = (f32[16,16,512]{1,0,2:T(8,128)S(1)}, f32[16,16,512]{1,0,2:T(8,128)}, u32[]{:S(2)}) copy-start(f32[16,16,512]{1,0,2:T(8,128)} %get-tuple-element.20) | copy-start | bytes 1572868
  240.8 6.4 %copy-start.23 = (f32[64,32,128]{2,1,0:T(8,128)S(1)}, f32[64,32,128]{2,1,0:T(8,128)}, u32[]{:S(2)}) copy-start(f32[64,32,128]{2,1,0:T(8,128)} %copy-done.22) | copy-start | bytes 3145732
  240.8 6.4 %copy-start.28 = (f32[64,32,128]{2,1,0:T(8,128)S(1)}, f32[64,32,128]{2,1,0:T(8,128)}, u32[]{:S(2)}) copy-start(f32[64,32,128]{2,1,0:T(8,128)} %get-tuple-element.105) | copy-start | bytes 3145732
  240.9 17.8 %all-to-all-start.2 = ((f32[8,1,32768]{2,1,0:T(1,128)}), f32[8,1,32768]{2,1,0:T(1,128)}, u32[]{:S(2)}, u32[]{:S(2)}) async-start(f32[8,1,32768]{2,1,0:T(1,128)} %reshape.301), calls=%async_computation.2 | async-start | bytes 2097152 | tf_op jit(solution)/shard_map/all_to_all | solution.py:151
  249.9 16.9 %copy-start.50 = (f32[16,64,128]{2,0,1:T(8,128)S(1)}, f32[16,64,128]{2,0,1:T(8,128)}, u32[]{:S(2)}) copy-start(f32[16,64,128]{2,0,1:T(8,128)} %copy-done.49) | copy-start | bytes 1572868
  249.9 16.9 %copy-start.52 = (f32[16,64,128]{2,0,1:T(8,128)S(1)}, f32[16,64,128]{2,0,1:T(8,128)}, u32[]{:S(2)}) copy-start(f32[16,64,128]{2,0,1:T(8,128)} %copy-done.51) | copy-start | bytes 1572868
  249.9 16.9 %copy-start.58 = (f32[16,64,128]{2,0,1:T(8,128)S(1)}, f32[16,64,128]{2,0,1:T(8,128)}, u32[]{:S(2)}) copy-start(f32[16,64,128]{2,0,1:T(8,128)} %copy-done.57) | copy-start | bytes 1572868
  249.9 16.9 %copy-start.62 = (f32[16,64,128]{2,0,1:T(8,128)S(1)}, f32[16,64,128]{2,0,1:T(8,128)}, u32[]{:S(2)}) copy-start(f32[16,64,128]{2,0,1:T(8,128)} %copy-done.61) | copy-start | bytes 1572868
  258.6 30.9 %all-to-all-start.4 = ((f32[64,32,128]{2,1,0:T(8,128)}), f32[64,32,128]{2,1,0:T(8,128)S(1)}, u32[]{:S(2)}, u32[]{:S(2)}) async-start(f32[64,32,128]{2,1,0:T(8,128)} %bitcast.98), calls=%async_computation.4 | async-start | bytes 2097152 | tf_op jit(solution)/shard_map/all_to_all | solution.py:157
  295.0 6.0 %collective-permute-start.7 = (f32[16,128,4]{1,0,2:T(8,128)S(1)}, f32[16,128,4]{1,0,2:T(8,128)S(1)}, u32[]{:S(2)}, u32[]{:S(2)}) collective-permute-start(f32[16,128,4]{1,0,2:T(8,128)S(1)} %copy.1319), channel_id=1, source_target_pairs={{0,4},{4,8},{8,12},{12,16},{16,20},{20,24},{24,28},{1,5},{5,9},{9,... | collective-permute-start | bytes 98312 | tf_op jit(solution)/shard_map/ppermute | solution.py:38
  297.4 5.2 collective-permute-start.8
  306.2 12.9 %collective-permute-start.9 = (f32[4,128,136]{2,0,1:T(4,128)}, f32[4,128,136]{2,0,1:T(4,128)}, u32[]{:S(2)}, u32[]{:S(2)}) collective-permute-start(f32[4,128,136]{2,0,1:T(4,128)} %get-tuple-element.59), channel_id=1, source_target_pairs={{0,1},{1,2},{2,3},{4,5},{5,6},{6,7},{8,9},{9,10},{10,11},{12,13},{... | collective-permute-start | bytes 835592 | tf_op jit(solution)/shard_map/ppermute | solution.py:38
  308.2 16.3 %collective-permute-start.10 = (f32[4,128,136]{2,0,1:T(4,128)}, f32[4,128,136]{2,0,1:T(4,128)}, u32[]{:S(2)}, u32[]{:S(2)}) collective-permute-start(f32[4,128,136]{2,0,1:T(4,128)} %get-tuple-element.60), channel_id=1, source_target_pairs={{1,0},{2,1},{3,2},{5,4},{6,5},{7,6},{9,8},{10,9},{11,10},{13,12},{... | collective-permute-start | bytes 835592 | tf_op jit(solution)/shard_map/ppermute | solution.py:41
  309.5 46.2 %all-to-all-start.5 = ((f32[16,128,128]{2,0,1:T(8,128)}), f32[16,128,128]{2,0,1:T(8,128)S(1)}, u32[]{:S(2)}, u32[]{:S(2)}) async-start(f32[16,128,128]{2,0,1:T(8,128)} %fusion.111), calls=%async_computation.5 | async-start | bytes 2097152 | tf_op jit(solution)/shard_map/all_to_all | solution.py:148
  346.8 13.7 %collective-permute-start.13 = (f32[16,32,128]{2,1,0:T(8,128)}, f32[16,32,128]{2,1,0:T(8,128)}, u32[]{:S(2)}, u32[]{:S(2)}) collective-permute-start(f32[16,32,128]{2,1,0:T(8,128)} %bitcast.312), channel_id=1, source_target_pairs={{0,3},{1,2},{2,1},{3,0},{4,7},{5,6},{6,5},{7,4},{8,11},{9,10},{10,... | collective-permute-start | bytes 786440 | tf_op jit(solution)/shard_map/ppermute | solution.py:28
  347.9 16.1 %collective-permute-start.11 = (f32[16,32,128]{2,1,0:T(8,128)}, f32[16,32,128]{2,1,0:T(8,128)}, u32[]{:S(2)}, u32[]{:S(2)}) collective-permute-start(f32[16,32,128]{2,1,0:T(8,128)} %bitcast.314), channel_id=1, source_target_pairs={{0,1},{1,0},{2,3},{3,2},{4,5},{5,4},{6,7},{7,6},{8,9},{9,8},{10,11... | collective-permute-start | bytes 786440 | tf_op jit(solution)/shard_map/ppermute | solution.py:28
  349.6 23.5 %collective-permute-start.12 = (f32[16,32,128]{2,1,0:T(8,128)}, f32[16,32,128]{2,1,0:T(8,128)}, u32[]{:S(2)}, u32[]{:S(2)}) collective-permute-start(f32[16,32,128]{2,1,0:T(8,128)} %bitcast.313), channel_id=1, source_target_pairs={{0,2},{1,3},{2,0},{3,1},{4,6},{5,7},{6,4},{7,5},{8,10},{9,11},{10,... | collective-permute-start | bytes 786440 | tf_op jit(solution)/shard_map/ppermute | solution.py:28
  355.7 35.0 %all-to-all-start.6 = ((f32[16,128,128]{2,0,1:T(8,128)}), f32[16,128,128]{2,0,1:T(8,128)S(1)}, u32[]{:S(2)}, u32[]{:S(2)}) async-start(f32[16,128,128]{2,0,1:T(8,128)} %get-tuple-element.57), calls=%async_computation.6 | async-start | bytes 2097152 | tf_op jit(solution)/shard_map/all_to_all | solution.py:147
  359.8 13.2 %copy-start.78 = (f32[16,2,2,128]{3,0,2,1:T(8,128)}, f32[16,2,2,128]{3,0,2,1:T(8,128)S(1)}, u32[]{:S(2)}) copy-start(f32[16,2,2,128]{3,0,2,1:T(8,128)S(1)} %copy.1323) | copy-start | bytes 98308
  390.7 129.9 %all-to-all-start.8 = ((f32[16,128,128]{2,0,1:T(8,128)}), f32[16,128,128]{2,0,1:T(8,128)}, u32[]{:S(2)}, u32[]{:S(2)}) async-start(f32[16,128,128]{2,0,1:T(8,128)} %fusion.111), calls=%async_computation.8 | async-start | bytes 2097152 | tf_op jit(solution)/shard_map/all_to_all | solution.py:154
  446.0 7.4 %copy-start.4 = (f32[16,16,512]{1,0,2:T(8,128)S(1)}, f32[16,16,512]{1,0,2:T(8,128)}, u32[]{:S(2)}) copy-start(f32[16,16,512]{1,0,2:T(8,128)} %get-tuple-element.18) | copy-start | bytes 1572868
  520.6 6.4 %copy-start.25 = (f32[64,32,128]{2,1,0:T(8,128)S(1)}, f32[64,32,128]{2,1,0:T(8,128)}, u32[]{:S(2)}) copy-start(f32[64,32,128]{2,1,0:T(8,128)} %copy-done.24) | copy-start | bytes 3145732
  520.6 6.4 %copy-start.27 = (f32[64,32,128]{2,1,0:T(8,128)S(1)}, f32[64,32,128]{2,1,0:T(8,128)}, u32[]{:S(2)}) copy-start(f32[64,32,128]{2,1,0:T(8,128)} %copy-done.26) | copy-start | bytes 3145732
  520.6 6.4 %copy-start.29 = (f32[64,32,128]{2,1,0:T(8,128)S(1)}, f32[64,32,128]{2,1,0:T(8,128)}, u32[]{:S(2)}) copy-start(f32[64,32,128]{2,1,0:T(8,128)} %get-tuple-element.91) | copy-start | bytes 3145732
  520.7 17.8 %all-to-all-start.7 = ((f32[8,1,32768]{2,1,0:T(1,128)}), f32[8,1,32768]{2,1,0:T(1,128)}, u32[]{:S(2)}, u32[]{:S(2)}) async-start(f32[8,1,32768]{2,1,0:T(1,128)} %reshape.303), calls=%async_computation.7 | async-start | bytes 2097152 | tf_op jit(solution)/shard_map/all_to_all | solution.py:151
  529.7 16.9 %copy-start.46 = (f32[16,64,128]{2,0,1:T(8,128)S(1)}, f32[16,64,128]{2,0,1:T(8,128)}, u32[]{:S(2)}) copy-start(f32[16,64,128]{2,0,1:T(8,128)} %copy-done.45) | copy-start | bytes 1572868
  529.7 16.9 %copy-start.48 = (f32[16,64,128]{2,0,1:T(8,128)S(1)}, f32[16,64,128]{2,0,1:T(8,128)}, u32[]{:S(2)}) copy-start(f32[16,64,128]{2,0,1:T(8,128)} %copy-done.47) | copy-start | bytes 1572868
  529.7 16.9 %copy-start.56 = (f32[16,64,128]{2,0,1:T(8,128)S(1)}, f32[16,64,128]{2,0,1:T(8,128)}, u32[]{:S(2)}) copy-start(f32[16,64,128]{2,0,1:T(8,128)} %copy-done.55) | copy-start | bytes 1572868
  529.7 16.9 %copy-start.60 = (f32[16,64,128]{2,0,1:T(8,128)S(1)}, f32[16,64,128]{2,0,1:T(8,128)}, u32[]{:S(2)}) copy-start(f32[16,64,128]{2,0,1:T(8,128)} %copy-done.59) | copy-start | bytes 1572868
  538.4 30.9 %all-to-all-start.9 = ((f32[64,32,128]{2,1,0:T(8,128)}), f32[64,32,128]{2,1,0:T(8,128)S(1)}, u32[]{:S(2)}, u32[]{:S(2)}) async-start(f32[64,32,128]{2,1,0:T(8,128)} %bitcast.199), calls=%async_computation.9 | async-start | bytes 2097152 | tf_op jit(solution)/shard_map/all_to_all | solution.py:157
  (70 other events, 158.8 us)
